TPU v7x, 256 devices: a whole 4x4x8 slice. The times are simulated.
256 devices in a mesh: layer: 4 (over x), row: 8 (over y, core), col: 8 (over z).
Axes of the slice: x: 4, y: 4, z: 8, core: 2. Of those that a mesh axis runs over, the one named last changes fastest.
Arguments:
- left_values: bfloat16 [8192, 4, 2048], P('row', 'layer', 'col'), may hold values from -22 to 22
- left_pattern: int32 [32, 4, 8], P('row', 'layer', 'col'), may hold values from 0 to 1, as said below
- right_values: bfloat16 [8192, 4, 2048], P(('layer', 'row'), None, 'col'), may hold values from -6 to 6
- right_pattern: int32 [32, 4, 8], P(('layer', 'row'), None, 'col'), may hold values from 0 to 1, as said below
Outputs:
- expanded: bfloat16 [8192, 4, 2048], P('row', 'layer', 'col')
Inputs may be any that keep to these rules, and one draw needn't show every extreme that they name: `left_pattern`: 1 marks a stored tile, 0 an absent one. `right_pattern`: 1 marks a stored tile, 0 an absent one.
All inputs are finite; a program needn't handle non-finite values.
Results may differ from a plain program's by a relative error of at most 0.001.
Values may be sent and summed in bfloat16 or wider, within the bound.
A program may use at most 64 MiB of HBM per device.

v0:
```python
import jax
import jax.numpy as jnp
from jax import lax
from jax.sharding import PartitionSpec as P


def expand_tiles(values, pattern):
    tile_rows, layers, tile_cols = pattern.shape
    tile_size = values.shape[0] // tile_rows
    blocks = values.reshape(tile_rows, tile_size, layers, tile_cols, tile_size)
    blocks = blocks * pattern[:, None, :, :, None].astype(values.dtype)
    return blocks.reshape(values.shape)


def per_device(left_values, left_pattern, right_values, right_pattern):
    left_block = expand_tiles(left_values, left_pattern)
    right_block = expand_tiles(right_values, right_pattern)
    rows_local = left_block.shape[0]
    columns_local = left_block.shape[2]
    left_flat = left_block.reshape(rows_local, columns_local)
    right_rows = lax.all_gather(right_block, "row", axis=0, tiled=True)
    right_mine = lax.all_to_all(right_rows, "layer", split_axis=1, concat_axis=0, tiled=True)
    right_mine = right_mine.reshape(right_mine.shape[0], columns_local)
    product = jnp.dot(
        lax.all_gather(left_flat, ("layer", "col"), axis=1, tiled=True),
        right_mine,
        preferred_element_type=jnp.float32,
    )
    product = product.reshape(rows_local, 1, columns_local)
    squared = product * product
    column = lax.psum(jnp.sum(squared, axis=0, keepdims=True), "row")
    rows_total = rows_local * lax.axis_size("row")
    colmean = column / rows_total
    return (squared / (colmean + 1e-06)).astype(jnp.bfloat16)


def solution(mesh):
    return jax.shard_map(
        per_device,
        mesh=mesh,
        in_specs=(
            P("row", "layer", "col"),
            P("row", "layer", "col"),
            P(("layer", "row"), None, "col"),
            P(("layer", "row"), None, "col"),
        ),
        out_specs=P("row", "layer", "col"),
        check_vma=False,
    )
```

profile of v0, /device:TPU:1, one launch (start us, length us, event | category | flops | bytes accessed | tf_op | source)
XLA Modules:
  0.0 238.1 jit_solution(10458258856644961506)
XLA Ops:
  6.5 0.0 all-gather.5.cloned.1.call-start
  6.5 0.7 convert_bitcast_fusion
  7.2 1.9 copy_multiply_fusion
  9.1 0.0 all-gather.5.cloned.1.call-update
  9.2 0.0 all-gather.3.cloned.1.call-start
  9.2 0.7 convert_bitcast_fusion.1
  9.9 0.1 broadcast_bitcast_fusion
  9.9 2.0 bitcast_multiply_fusion
  12.0 0.0 all-gather.3.cloned.1.call-update
  12.0 36.2 %all-gather.5.cloned.1.call-done = bf16[2048,4,256]{2,0,1:T(8,128)(2,1)} async-done(((bf16[256,4,256]{2,0,1:T(8,128)(2,1)}), bf16[2048,4,256]{2,0,1:T(8,128)(2,1)}) %all-gather.5.cloned.1.call-update) | async-done | bytes 4194320 | tf_op jit(solution)/shard_map/all_gather | solution.py:21
  48.2 62.8 %all_to_all.15 = bf16[2048,4,256]{2,0,1:T(8,128)(2,1)} all-to-all(bf16[2048,4,256]{2,0,1:T(8,128)(2,1)} %all-gather.5.cloned.1.call-done), channel_id=1, replica_groups=mesh['layer'=4,'row'=8,'col'=8] {'layer'}, dimensions={1} | all-to-all | bytes 8388608 | tf_op jit(solution)/shard_map/all_to_all | solution.py:22
  111.0 95.2 %all-gather.3.cloned.1.call-done = bf16[1024,8192]{1,0:T(8,128)(2,1)} async-done(((bf16[1024,256]{1,0:T(8,128)(2,1)}), bf16[1024,8192]{1,0:T(8,128)(2,1)}) %all-gather.3.cloned.1.call-update) | async-done | bytes 16777232 | tf_op jit(solution)/shard_map/all_gather | solution.py:25
  206.1 9.3 %fusion.1 = (f32[256]{0:T(256)S(1)}, f32[1024,256]{1,0:T(8,128)S(1)}) fusion(bf16[1024,8192]{1,0:T(8,128)(2,1)} %all-gather.3.cloned.1.call-done, bf16[8192,256]{1,0:T(8,128)(2,1)} %bitcast.20), kind=kOutput, calls=%fused_computation.9 | convolution fusion | flops 4295491584 | bytes 22021120 | tf_op jit(solution)/shard_map/dot_general | solution.py:24
  215.5 14.9 %psum.7 = f32[1,1,256]{2,1,0:T(1,128)S(1)} all-reduce(f32[1,1,256]{2,1,0:T(1,128)S(1)} %bitcast.23), channel_id=1, replica_groups=mesh['layer'=4,'row'=8,'col'=8] {'row'}, use_global_device_ids=true, to_apply=%region_1.0 | all-reduce | flops 256 | bytes 2048 | tf_op jit(solution)/shard_map/psum | solution.py:31
  230.4 0.9 fusion
  (2 shorter events, 0.0 us)
Async XLA Ops:
  6.5 41.7 %all-gather.5.cloned.1.call-start = ((), (), s32[]{:S(2)}) async-start(), calls=%async_computation.2 | async-start | bytes 4718592 | tf_op jit(solution)/shard_map/all_gather | solution.py:21
  9.2 197.0 %all-gather.3.cloned.1.call-start = ((), (), s32[]{:S(2)}) async-start(), calls=%async_computation.1 | async-start | bytes 17301504 | tf_op jit(solution)/shard_map/all_gather | solution.py:25
Sparse Core Ops, SparseCore 0:
  9.3 38.8 all-gather.4
  50.7 155.4 all-gather.2
where the time goes:
time: 238 us
  waiting for transfers between devices  131 us (55%)
  blocking collectives  77.7 us (33%)
  between operations  13.4 us (6%)
  matrix products  9.32 us (4%)
  other arithmetic  6.17 us (3%)
    all_gather x1, waiting for transfers between devices, per_device(): lax.all_gather(left_flat, ('layer', 'col'), axis=1, tiled=True)  95.2 us
    all_to_all x1, blocking collectives, per_device(): lax.all_to_all(right_rows, 'layer', split_axis=1, concat_axis=0, tiled=True)  62.8 us
    all_gather x1, waiting for transfers between devices, per_device(): right_rows = lax.all_gather(right_block, 'row', axis=0, tiled=True)  36.2 us
    psum x1, blocking collectives, per_device(): column = lax.psum(jnp.sum(squared, axis=0, keepdims=True), 'row')  14.9 us
    dot_general x1, matrix products, per_device(): jnp.dot(lax.all_gather(left_flat, ('layer', 'col'), axis=1, tiled=True),...  9.32 us
  transfers between devices with their start and end apart: 2, of which 2 were waited for; matrix products, arithmetic and copies ran while one was open for 1% of the time, Pallas kernels for 0%

commit v1 on v0

--- a/solution.py
+++ b/solution.py
@@ -2,6 +2,10 @@
 import jax.numpy as jnp
 from jax import lax
 from jax.sharding import PartitionSpec as P
+
+
+def fix_the_slices(sample, a_name):
+    return lax.all_gather(sample, a_name).sum(axis=0)
 
 
 def expand_tiles(values, pattern):
@@ -28,7 +32,7 @@
     )
     product = product.reshape(rows_local, 1, columns_local)
     squared = product * product
-    column = lax.psum(jnp.sum(squared, axis=0, keepdims=True), "row")
+    column = fix_the_slices(jnp.sum(squared, axis=0, keepdims=True), "row")
     rows_total = rows_local * lax.axis_size("row")
     colmean = column / rows_total
     return (squared / (colmean + 1e-06)).astype(jnp.bfloat16)

time: 238 us -> 237 us (level)
    psum x1 -> x0, blocking collectives: 14.9 us -> none  [per_device(): column = lax.psum(jnp.sum(squared, axis=0, keepdims=True), 'row')]
    all_gather x0 -> x1, blocking collectives: none -> 13.5 us  [fix_the_slices(): return lax.all_gather(sample, a_name).sum(axis=0)]
where the time goes in v1:
time: 237 us
  waiting for transfers between devices  131 us (55%)
  blocking collectives  76.2 us (32%)
  between operations  13.4 us (6%)
  matrix products  9.32 us (4%)
  other arithmetic  6.2 us (3%)
    all_gather x1, waiting for transfers between devices, per_device(): lax.all_gather(left_flat, ('layer', 'col'), axis=1, tiled=True)  95.2 us
    all_to_all x1, blocking collectives, per_device(): lax.all_to_all(right_rows, 'layer', split_axis=1, concat_axis=0, tiled=True)  62.8 us
    all_gather x1, waiting for transfers between devices, per_device(): right_rows = lax.all_gather(right_block, 'row', axis=0, tiled=True)  36.2 us
    all_gather x1, blocking collectives, fix_the_slices(): return lax.all_gather(sample, a_name).sum(axis=0)  13.5 us
    dot_general x1, matrix products, per_device(): jnp.dot(lax.all_gather(left_flat, ('layer', 'col'), axis=1, tiled=True),...  9.32 us
  transfers between devices with their start and end apart: 2, of which 2 were waited for; matrix products, arithmetic and copies ran while one was open for 1% of the time, Pallas kernels for 0%

profile of v1, /device:TPU:1, one launch (start us, length us, event | category | flops | bytes accessed | tf_op | source)
XLA Modules:
  0.0 236.7 jit_solution(14618837574521213013)
XLA Ops:
  6.5 0.0 all-gather.7.cloned.1.call-start
  6.5 0.7 convert_bitcast_fusion
  7.2 1.9 copy_multiply_fusion
  9.1 0.0 all-gather.7.cloned.1.call-update
  9.2 0.0 all-gather.5.cloned.1.call-start
  9.2 0.7 convert_bitcast_fusion.1
  9.9 0.1 broadcast_bitcast_fusion
  9.9 2.0 bitcast_multiply_fusion
  12.0 0.0 all-gather.5.cloned.1.call-update
  12.0 36.2 %all-gather.7.cloned.1.call-done = bf16[2048,4,256]{2,0,1:T(8,128)(2,1)} async-done(((bf16[256,4,256]{2,0,1:T(8,128)(2,1)}), bf16[2048,4,256]{2,0,1:T(8,128)(2,1)}) %all-gather.7.cloned.1.call-update) | async-done | bytes 4194320 | tf_op jit(solution)/shard_map/all_gather | solution.py:25
  48.2 62.8 %all_to_all.15 = bf16[2048,4,256]{2,0,1:T(8,128)(2,1)} all-to-all(bf16[2048,4,256]{2,0,1:T(8,128)(2,1)} %all-gather.7.cloned.1.call-done), channel_id=1, replica_groups=mesh['layer'=4,'row'=8,'col'=8] {'layer'}, dimensions={1} | all-to-all | bytes 8388608 | tf_op jit(solution)/shard_map/all_to_all | solution.py:26
  111.0 95.2 %all-gather.5.cloned.1.call-done = bf16[1024,8192]{1,0:T(8,128)(2,1)} async-done(((bf16[1024,256]{1,0:T(8,128)(2,1)}), bf16[1024,8192]{1,0:T(8,128)(2,1)}) %all-gather.5.cloned.1.call-update) | async-done | bytes 16777232 | tf_op jit(solution)/shard_map/all_gather | solution.py:29
  206.1 9.3 %fusion.1 = (f32[256]{0:T(256)S(1)}, f32[1024,256]{1,0:T(8,128)S(1)}) fusion(bf16[1024,8192]{1,0:T(8,128)(2,1)} %all-gather.5.cloned.1.call-done, bf16[8192,256]{1,0:T(8,128)(2,1)} %bitcast.19), kind=kOutput, calls=%fused_computation.9 | convolution fusion | flops 4295491584 | bytes 22021120 | tf_op jit(solution)/shard_map/dot_general | solution.py:28
  215.5 13.5 %all-gather.1 = f32[8,1,256]{2,1,0:T(1,128)S(1)} all-gather(f32[1,1,256]{2,1,0:T(1,128)S(1)} %bitcast.21), channel_id=2, replica_groups=mesh['layer'=4,'row'=8,'col'=8] {'row'}, dimensions={0}, use_global_device_ids=true | all-gather | bytes 9216 | tf_op jit(solution)/shard_map/all_gather | solution.py:8
  229.0 0.9 fusion
  (3 shorter events, 0.0 us)
Async XLA Ops:
  6.5 41.7 %all-gather.7.cloned.1.call-start = ((), (), s32[]{:S(2)}) async-start(), calls=%async_computation.2 | async-start | bytes 4718592 | tf_op jit(solution)/shard_map/all_gather | solution.py:25
  9.2 197.0 %all-gather.5.cloned.1.call-start = ((), (), s32[]{:S(2)}) async-start(), calls=%async_computation.1 | async-start | bytes 17301504 | tf_op jit(solution)/shard_map/all_gather | solution.py:29
Sparse Core Ops, SparseCore 0:
  9.3 38.8 all-gather.6
  50.7 155.4 all-gather.4

commit v2 on v0

--- a/solution.py
+++ b/solution.py
@@ -2,6 +2,12 @@
 import jax.numpy as jnp
 from jax import lax
 from jax.sharding import PartitionSpec as P
+
+
+def view_widths_by_axis(shard_in, row_dim):
+    shard_in = jnp.moveaxis(shard_in, 0, row_dim)
+    big = shard_in.shape
+    return shard_in.reshape(*big[:row_dim], big[row_dim] * big[row_dim + 1], *big[row_dim + 2 :])
 
 
 def expand_tiles(values, pattern):
@@ -18,7 +24,27 @@
     rows_local = left_block.shape[0]
     columns_local = left_block.shape[2]
     left_flat = left_block.reshape(rows_local, columns_local)
-    right_rows = lax.all_gather(right_block, "row", axis=0, tiled=True)
+    n_slots = lax.psum(1, axis_name="row")
+    panels = []
+    for t in range(n_slots):
+        panels.append((t, (t + 1) % n_slots))
+    pool = []
+    for dev, kk in panels:
+        pool.append((kk, dev))
+    local_now, parts_out = ([], [])
+    for rr in range(n_slots - 1):
+        if rr % 2 == 0:
+            outer = lax.ppermute(local_now[-1] if local_now else right_block, "row", perm=panels)
+            local_now.append(outer)
+        else:
+            o_now = lax.ppermute(parts_out[-1] if parts_out else right_block, "row", perm=pool)
+            parts_out.append(o_now)
+    raw_out = jnp.stack([*local_now[::-1], right_block, *parts_out], 0)
+    view_out = lax.axis_index("row")
+    e_now = len(local_now)
+    piece_next = view_out - e_now
+    raw_out = raw_out[(jnp.arange(n_slots) - piece_next) % n_slots]
+    right_rows = view_widths_by_axis(raw_out, 0)
     right_mine = lax.all_to_all(right_rows, "layer", split_axis=1, concat_axis=0, tiled=True)
     right_mine = right_mine.reshape(right_mine.shape[0], columns_local)
     product = jnp.dot(

time: 238 us -> 238 us (level)
  waiting for transfers between devices: 131 us -> 86.5 us
  local copies, waits for them, and re-layouts: 0.08 us -> 18.5 us
  starting transfers between devices: 0.04 us -> 18 us
  blocking collectives: 77.7 us -> 84.9 us
    all_gather x1 -> x0, waiting for transfers between devices: 36.2 us -> none  [per_device(): right_rows = lax.all_gather(right_block, 'row', axis=0, tiled=True)]
    all_gather x1, waiting for transfers between devices: 95.2 us -> 69.8 us  [per_device(): lax.all_gather(left_flat, ('layer', 'col'), axis=1, tiled=True)]
    ppermute x0 -> x7, starting transfers between devices: none -> 18 us  [the longest x4 10.1 us: per_device(): lax.ppermute(local_now[-1] if local_now else right_block, 'row', perm=pan...]
    ppermute x0 -> x7, waiting for transfers between devices: none -> 16.7 us  [the longest x4 15.5 us: per_device(): lax.ppermute(local_now[-1] if local_now else right_block, 'row', perm=pan...]
    gather x0 -> x2, local copies, waits for them, and re-layouts: none -> 10.5 us  [per_device(): raw_out = raw_out[(jnp.arange(n_slots) - piece_next) % n_slots]]
    all_to_all x1, blocking collectives: 62.8 us -> 71.4 us  [per_device(): lax.all_to_all(right_rows, 'layer', split_axis=1, concat_axis=0, tiled=True)]
    unnamed x2 -> x10, local copies, waits for them, and re-layouts: 0.08 us -> 7 us
  transfers between devices with their start and end apart: 2 -> 8, of which waited for: 2 -> 7; matrix products, arithmetic and copies ran while one was open for 1% -> 9% of each run, Pallas kernels for 0% -> 0%
where the time goes in v2:
time: 238 us; the launch traced here: 237 us
  waiting for transfers between devices  86.5 us (36%)
  blocking collectives  84.9 us (36%)
  local copies, waits for them, and re-layouts  18.5 us (8%)
  starting transfers between devices  18 us (8%)
  between operations  13.4 us (6%)
  matrix products  9.32 us (4%)
  other arithmetic  6.71 us (3%)
    all_to_all x1, blocking collectives, per_device(): lax.all_to_all(right_rows, 'layer', split_axis=1, concat_axis=0, tiled=True)  71.4 us
    all_gather x1, waiting for transfers between devices, per_device(): lax.all_gather(left_flat, ('layer', 'col'), axis=1, tiled=True)  69.8 us
    ppermute x4, waiting for transfers between devices, per_device(): lax.ppermute(local_now[-1] if local_now else right_block, 'row', perm=pan...  15.5 us
    psum x1, blocking collectives, per_device(): column = lax.psum(jnp.sum(squared, axis=0, keepdims=True), 'row')  13.5 us
    gather x2, local copies, waits for them, and re-layouts, per_device(): raw_out = raw_out[(jnp.arange(n_slots) - piece_next) % n_slots]  10.5 us
    ppermute x4, starting transfers between devices, per_device(): lax.ppermute(local_now[-1] if local_now else right_block, 'row', perm=pan...  10.1 us
    dot_general x1, matrix products, per_device(): jnp.dot(lax.all_gather(left_flat, ('layer', 'col'), axis=1, tiled=True),...  9.32 us
    ppermute x3, starting transfers between devices, per_device(): lax.ppermute(parts_out[-1] if parts_out else right_block, 'row', perm=pool)  7.82 us
  transfers between devices with their start and end apart: 8, of which 7 were waited for; matrix products, arithmetic and copies ran while one was open for 9% of the time, Pallas kernels for 0%

profile of v2, /device:TPU:1, one launch (start us, length us, event | category | flops | bytes accessed | tf_op | source)
XLA Modules:
  0.0 237.3 jit_solution(16741400687153011279)
XLA Ops:
  7.3 2.0 bitcast_multiply_fusion
  10.1 1.3 broadcast_multiply_fusion
  11.4 2.7 %collective-permute-start = (bf16[256,4,256]{2,1,0:T(4,128)(2,1)S(1)}, bf16[256,4,256]{2,1,0:T(4,128)(2,1)S(1)}, u32[]{:S(2)}, u32[]{:S(2)}) collective-permute-start(bf16[256,4,256]{2,1,0:T(4,128)(2,1)S(1)} %broadcast_multiply_fusion), channel_id=1, source_target_pairs={{0,8},{8,16},{16,24},{24,32},{32,40},{40,48},{48,56},{56,0},{1,9},... | collective-permute-start | bytes 1572872 | tf_op jit(solution)/shard_map/ppermute | solution.py:37
  14.1 6.1 %collective-permute-done = bf16[256,4,256]{2,1,0:T(4,128)(2,1)S(1)} collective-permute-done((bf16[256,4,256]{2,1,0:T(4,128)(2,1)S(1)}, bf16[256,4,256]{2,1,0:T(4,128)(2,1)S(1)}, u32[]{:S(2)}, u32[]{:S(2)}) %collective-permute-start) | collective-permute-done | bytes 524320 | tf_op jit(solution)/shard_map/ppermute | solution.py:37
  20.2 2.5 %collective-permute-start.1 = (bf16[256,4,256]{2,1,0:T(4,128)(2,1)S(1)}, bf16[256,4,256]{2,1,0:T(4,128)(2,1)S(1)}, u32[]{:S(2)}, u32[]{:S(2)}) collective-permute-start(bf16[256,4,256]{2,1,0:T(4,128)(2,1)S(1)} %collective-permute-done), channel_id=1, source_target_pairs={{0,8},{8,16},{16,24},{24,32},{32,40},{40,48},{48,56},{56,0},{1,9},... | collective-permute-start | bytes 1572872 | tf_op jit(solution)/shard_map/ppermute | solution.py:37
  22.7 1.8 collective-permute-start.4
  24.5 4.4 %collective-permute-done.1 = bf16[256,4,256]{2,1,0:T(4,128)(2,1)S(1)} collective-permute-done((bf16[256,4,256]{2,1,0:T(4,128)(2,1)S(1)}, bf16[256,4,256]{2,1,0:T(4,128)(2,1)S(1)}, u32[]{:S(2)}, u32[]{:S(2)}) %collective-permute-start.1) | collective-permute-done | bytes 524320 | tf_op jit(solution)/shard_map/ppermute | solution.py:37
  28.8 2.5 %collective-permute-start.2 = (bf16[256,4,256]{2,1,0:T(4,128)(2,1)S(1)}, bf16[256,4,256]{2,1,0:T(4,128)(2,1)S(1)}, u32[]{:S(2)}, u32[]{:S(2)}) collective-permute-start(bf16[256,4,256]{2,1,0:T(4,128)(2,1)S(1)} %collective-permute-done.1), channel_id=1, source_target_pairs={{0,8},{8,16},{16,24},{24,32},{32,40},{40,48},{48,56},{56,0},{1,9},... | collective-permute-start | bytes 1572872 | tf_op jit(solution)/shard_map/ppermute | solution.py:37
  31.7 2.6 %collective-permute-start.5 = (bf16[256,4,256]{2,1,0:T(4,128)(2,1)S(1)}, bf16[256,4,256]{2,1,0:T(4,128)(2,1)S(1)}, u32[]{:S(2)}, u32[]{:S(2)}) collective-permute-start(bf16[256,4,256]{2,1,0:T(4,128)(2,1)S(1)} %collective-permute-done.4), channel_id=1, source_target_pairs={{8,0},{16,8},{24,16},{32,24},{40,32},{48,40},{56,48},{0,56},{9,1},... | collective-permute-start | bytes 1572872 | tf_op jit(solution)/shard_map/ppermute | solution.py:40
  34.3 3.1 %collective-permute-done.2 = bf16[256,4,256]{2,1,0:T(4,128)(2,1)S(1)} collective-permute-done((bf16[256,4,256]{2,1,0:T(4,128)(2,1)S(1)}, bf16[256,4,256]{2,1,0:T(4,128)(2,1)S(1)}, u32[]{:S(2)}, u32[]{:S(2)}) %collective-permute-start.2) | collective-permute-done | bytes 524320 | tf_op jit(solution)/shard_map/ppermute | solution.py:37
  37.4 2.5 %collective-permute-start.3 = (bf16[256,4,256]{2,1,0:T(4,128)(2,1)S(1)}, bf16[256,4,256]{2,1,0:T(4,128)(2,1)}, u32[]{:S(2)}, u32[]{:S(2)}) collective-permute-start(bf16[256,4,256]{2,1,0:T(4,128)(2,1)S(1)} %collective-permute-done.2), channel_id=1, source_target_pairs={{0,8},{8,16},{16,24},{24,32},{32,40},{40,48},{48,56},{56,0},{1,9},... | collective-permute-start | bytes 1572872 | tf_op jit(solution)/shard_map/ppermute | solution.py:37
  40.7 3.5 %collective-permute-start.6 = (bf16[256,4,256]{2,1,0:T(4,128)(2,1)S(1)}, bf16[256,4,256]{2,1,0:T(4,128)(2,1)S(1)}, u32[]{:S(2)}, u32[]{:S(2)}) collective-permute-start(bf16[256,4,256]{2,1,0:T(4,128)(2,1)S(1)} %collective-permute-done.5), channel_id=1, source_target_pairs={{8,0},{16,8},{24,16},{32,24},{40,32},{48,40},{56,48},{0,56},{9,1},... | collective-permute-start | bytes 1572872 | tf_op jit(solution)/shard_map/ppermute | solution.py:40
  44.2 1.9 collective-permute-done.3
  46.0 2.0 bitcast_dynamic-update-slice_fusion.7
  49.0 1.0 bitcast_dynamic-update-slice_fusion.5
  50.0 1.0 bitcast_dynamic-update-slice_fusion.4
  51.0 1.1 bitcast_dynamic-update-slice_fusion.3
  52.1 1.0 bitcast_dynamic-update-slice_fusion.2
  55.0 7.6 %gather_fusion = bf16[8,256,4,256]{3,2,1,0:T(4,128)(2,1)} fusion(bf16[8,256,4,256]{3,2,1,0:T(4,128)(2,1)} %bitcast_dynamic-update-slice_fusion, s32[1024]{0:T(1024)S(1)} %pad_clamp_fusion), kind=kCustom, calls=%fused_computation | custom fusion | bytes 8388640 | tf_op jit(solution)/shard_map/gather | solution.py:46
  62.6 2.9 %copy.5 = bf16[8,256,4,256]{3,1,0,2:T(8,128)(2,1)S(1)} copy(bf16[8,256,4,256]{3,2,1,0:T(4,128)(2,1)} %gather_fusion) | data formatting | bytes 8388608 | tf_op jit(solution)/shard_map/gather | solution.py:46
  65.5 71.4 %all_to_all.15 = bf16[2048,4,256]{2,0,1:T(8,128)(2,1)} all-to-all(bf16[2048,4,256]{2,0,1:T(8,128)(2,1)S(1)} %bitcast.39), channel_id=1, replica_groups=mesh['layer'=4,'row'=8,'col'=8] {'layer'}, dimensions={1} | all-to-all | bytes 8388608 | tf_op jit(solution)/shard_map/all_to_all | solution.py:48
  136.9 69.8 %all-gather.2.cloned.1.call-done = bf16[1024,8192]{1,0:T(8,128)(2,1)} async-done(((bf16[1024,256]{1,0:T(8,128)(2,1)}), bf16[1024,8192]{1,0:T(8,128)(2,1)}) %all-gather.2.cloned.1.call-update) | async-done | bytes 16777232 | tf_op jit(solution)/shard_map/all_gather | solution.py:51
  206.7 9.3 %fusion.3 = (f32[256]{0:T(256)S(1)}, f32[1024,256]{1,0:T(8,128)S(1)}) fusion(bf16[1024,8192]{1,0:T(8,128)(2,1)} %all-gather.2.cloned.1.call-done, bf16[8192,256]{1,0:T(8,128)(2,1)} %bitcast.40), kind=kOutput, calls=%fused_computation.25 | convolution fusion | flops 4295491584 | bytes 22021120 | tf_op jit(solution)/shard_map/dot_general | solution.py:50
  216.1 13.5 %psum.7 = f32[1,1,256]{2,1,0:T(1,128)S(1)} all-reduce(f32[1,1,256]{2,1,0:T(1,128)S(1)} %bitcast.43), channel_id=1, replica_groups=mesh['layer'=4,'row'=8,'col'=8] {'row'}, use_global_device_ids=true, to_apply=%region_1.2 | all-reduce | flops 256 | bytes 2048 | tf_op jit(solution)/shard_map/psum | solution.py:57
  (18 shorter events, 6.4 us)
Async XLA Ops:
  6.5 44.5 %copy-start = (bf16[256,4,256]{2,1,0:T(4,128)(2,1)S(1)}, bf16[256,4,256]{2,1,0:T(4,128)(2,1)}, u32[]{:S(2)}) copy-start(bf16[256,4,256]{2,1,0:T(4,128)(2,1)} %param.6) | copy-start | bytes 1572868
  6.5 200.2 %all-gather.2.cloned.1.call-start = ((), (), s32[]{:S(2)}) async-start(), calls=%async_computation.1 | async-start | bytes 17301504 | tf_op jit(solution)/shard_map/all_gather | solution.py:51
  11.4 8.8 %collective-permute-start = (bf16[256,4,256]{2,1,0:T(4,128)(2,1)S(1)}, bf16[256,4,256]{2,1,0:T(4,128)(2,1)S(1)}, u32[]{:S(2)}, u32[]{:S(2)}) collective-permute-start(bf16[256,4,256]{2,1,0:T(4,128)(2,1)S(1)} %broadcast_multiply_fusion), channel_id=1, source_target_pairs={{0,8},{8,16},{16,24},{24,32},{32,40},{40,48},{48,56},{56,0},{1,9},... | collective-permute-start | bytes 1572872 | tf_op jit(solution)/shard_map/ppermute | solution.py:37
  20.2 8.6 %collective-permute-start.1 = (bf16[256,4,256]{2,1,0:T(4,128)(2,1)S(1)}, bf16[256,4,256]{2,1,0:T(4,128)(2,1)S(1)}, u32[]{:S(2)}, u32[]{:S(2)}) collective-permute-start(bf16[256,4,256]{2,1,0:T(4,128)(2,1)S(1)} %collective-permute-done), channel_id=1, source_target_pairs={{0,8},{8,16},{16,24},{24,32},{32,40},{40,48},{48,56},{56,0},{1,9},... | collective-permute-start | bytes 1572872 | tf_op jit(solution)/shard_map/ppermute | solution.py:37
  22.7 9.0 %collective-permute-start.4 = (bf16[256,4,256]{2,1,0:T(4,128)(2,1)S(1)}, bf16[256,4,256]{2,1,0:T(4,128)(2,1)S(1)}, u32[]{:S(2)}, u32[]{:S(2)}) collective-permute-start(bf16[256,4,256]{2,1,0:T(4,128)(2,1)S(1)} %broadcast_multiply_fusion), channel_id=1, source_target_pairs={{8,0},{16,8},{24,16},{32,24},{40,32},{48,40},{56,48},{0,56},{9,1},... | collective-permute-start | bytes 1572872 | tf_op jit(solution)/shard_map/ppermute | solution.py:40
  28.8 8.6 %collective-permute-start.2 = (bf16[256,4,256]{2,1,0:T(4,128)(2,1)S(1)}, bf16[256,4,256]{2,1,0:T(4,128)(2,1)S(1)}, u32[]{:S(2)}, u32[]{:S(2)}) collective-permute-start(bf16[256,4,256]{2,1,0:T(4,128)(2,1)S(1)} %collective-permute-done.1), channel_id=1, source_target_pairs={{0,8},{8,16},{16,24},{24,32},{32,40},{40,48},{48,56},{56,0},{1,9},... | collective-permute-start | bytes 1572872 | tf_op jit(solution)/shard_map/ppermute | solution.py:37
  31.7 9.0 %collective-permute-start.5 = (bf16[256,4,256]{2,1,0:T(4,128)(2,1)S(1)}, bf16[256,4,256]{2,1,0:T(4,128)(2,1)S(1)}, u32[]{:S(2)}, u32[]{:S(2)}) collective-permute-start(bf16[256,4,256]{2,1,0:T(4,128)(2,1)S(1)} %collective-permute-done.4), channel_id=1, source_target_pairs={{8,0},{16,8},{24,16},{32,24},{40,32},{48,40},{56,48},{0,56},{9,1},... | collective-permute-start | bytes 1572872 | tf_op jit(solution)/shard_map/ppermute | solution.py:40
  37.4 8.6 %collective-permute-start.3 = (bf16[256,4,256]{2,1,0:T(4,128)(2,1)S(1)}, bf16[256,4,256]{2,1,0:T(4,128)(2,1)}, u32[]{:S(2)}, u32[]{:S(2)}) collective-permute-start(bf16[256,4,256]{2,1,0:T(4,128)(2,1)S(1)} %collective-permute-done.2), channel_id=1, source_target_pairs={{0,8},{8,16},{16,24},{24,32},{32,40},{40,48},{48,56},{56,0},{1,9},... | collective-permute-start | bytes 1572872 | tf_op jit(solution)/shard_map/ppermute | solution.py:37
  40.7 13.4 %collective-permute-start.6 = (bf16[256,4,256]{2,1,0:T(4,128)(2,1)S(1)}, bf16[256,4,256]{2,1,0:T(4,128)(2,1)S(1)}, u32[]{:S(2)}, u32[]{:S(2)}) collective-permute-start(bf16[256,4,256]{2,1,0:T(4,128)(2,1)S(1)} %collective-permute-done.5), channel_id=1, source_target_pairs={{8,0},{16,8},{24,16},{32,24},{40,32},{48,40},{56,48},{0,56},{9,1},... | collective-permute-start | bytes 1572872 | tf_op jit(solution)/shard_map/ppermute | solution.py:40
Sparse Core Ops, SparseCore 0:
  9.8 196.8 all-gather.1
